TPU v7x, 256 devices: a whole 4x4x8 slice. The times are simulated.
256 devices in a mesh: kv: 4 (over y), seq: 64 (over z, x, core).
Axes of the slice: x: 4, y: 4, z: 8, core: 2. Of those that a mesh axis runs over, the one named last changes fastest.
Arguments:
- sampled_rows: int32 [6144], replicated, may hold values from 0 to 16383, as said below
- query_vectors: bfloat16 [6144, 64, 128], P('seq', 'kv'), may hold values from -150 to 150
- key_vectors: bfloat16 [16384, 8, 128], P('seq', 'kv'), may hold values from -6 to 6
Outputs:
- heavy_hitters: float32 [16384], P('seq')
Inputs may be any that keep to these rules, and one draw needn't show every extreme that they name: `sampled_rows`: strictly increasing sequence positions.
All inputs are finite; a program needn't handle non-finite values.
Results may differ from a plain program's by a relative error of at most 0.0003.
Values may be sent and summed in bfloat16 or wider, within the bound.
A program may use at most 64 MiB of HBM per device.

v0:
```python
import math
import jax
import jax.numpy as jnp
from jax import lax
from jax.sharding import PartitionSpec as P

HD = 128
NEG = -1e30


def split_up(array, dim, devices):
    before, after = (array.shape[:dim], array.shape[dim + 1 :])
    return jnp.moveaxis(array.reshape(*before, devices, -1, *after), dim, 0)


def sum_at_owner(array, axis, dim):
    devices = lax.axis_size(axis)
    tiles = lax.all_to_all(split_up(array, dim, devices), axis, 0, 0, tiled=True)
    return jnp.sum(tiles, axis=0)


def copy_for_each(array, axis):
    copies = jnp.broadcast_to(array, (lax.axis_size(axis), *array.shape))
    return lax.all_to_all(copies, axis, split_axis=0, concat_axis=0, tiled=True)


def of_everyone(array, axis):
    return copy_for_each(array, axis).sum(axis=0)


def block_scores(query_block, key_block, factor):
    return (
        jnp.einsum("rgid,kgd->rgik", query_block, key_block, preferred_element_type=jnp.float32)
        * factor
    )


def visibility(rows_block, offset, amount):
    places = offset + jnp.arange(amount, dtype=jnp.int32)
    return places[None, None, None, :] <= rows_block[:, None, None, None]


def stats_block(query_block, rows_block, key_block, offset, running, factor):
    row_max, row_total = running
    scores = block_scores(query_block, key_block, factor)
    visible = visibility(rows_block, offset, key_block.shape[0])
    scores = jnp.where(visible, scores, NEG)
    new_max = jnp.maximum(row_max, jnp.max(scores, axis=-1))
    terms = jnp.where(visible, jnp.exp(scores - new_max[..., None]), 0.0)
    return (new_max, row_total * jnp.exp(row_max - new_max) + jnp.sum(terms, axis=-1))


def prob_columns(query_block, rows_block, key_block, offset, log_total, factor):
    scores = block_scores(query_block, key_block, factor)
    visible = visibility(rows_block, offset, key_block.shape[0])
    probability = jnp.where(visible, jnp.exp(scores - log_total[..., None]), 0.0)
    return jnp.sum(probability, axis=(0, 1, 2))


def on_device(sampled_rows, query_vectors, key_vectors):
    local_rows = query_vectors.shape[0]
    local_keys = key_vectors.shape[0]
    local_groups = key_vectors.shape[1]
    group_size = query_vectors.shape[1] // local_groups
    factor = 1.0 / math.sqrt(HD)
    seq_index = lax.axis_index("seq")
    grouped = query_vectors.reshape(local_rows, local_groups, group_size, HD)
    own_rows = lax.dynamic_slice_in_dim(sampled_rows, seq_index * local_rows, local_rows, 0)
    highest = jnp.max(own_rows)
    gathered = lax.all_gather(key_vectors, "seq", axis=0, tiled=True)
    total_keys = gathered.shape[0]
    key_stride = math.gcd(total_keys, 2048)

    def sweep(running, key_index):
        offset = key_index * key_stride

        def sweep_active(state):
            key_block = lax.dynamic_slice_in_dim(gathered, offset, key_stride, 0)
            return stats_block(grouped, own_rows, key_block, offset, state, factor)

        return (lax.cond(offset <= highest, sweep_active, lambda state: state, running), None)

    initial = (
        jnp.full((local_rows, local_groups, group_size), NEG, jnp.float32),
        jnp.zeros((local_rows, local_groups, group_size), jnp.float32),
    )
    (row_max, row_total), _ = lax.scan(
        sweep, initial, jnp.arange(total_keys // key_stride, dtype=jnp.int32)
    )
    log_total = row_max + jnp.log(row_total)

    def terms(offset, amount):
        stride = math.gcd(amount, 2048)

        def portion(block_index):
            first = block_index * stride

            def portion_active():
                key_block = lax.dynamic_slice_in_dim(gathered, first, stride, 0)
                return prob_columns(grouped, own_rows, key_block, first, log_total, factor)

            return lax.cond(
                first <= highest, portion_active, lambda: jnp.zeros((stride,), jnp.float32)
            )

        return lax.map(portion, jnp.arange(amount // stride, dtype=jnp.int32)).reshape(amount)

    columns = sum_at_owner(terms(jnp.int32(0), local_keys * lax.axis_size("seq")), "seq", 0)
    summed = of_everyone(columns, "kv")
    return summed * (1.0 / group_size)


def solution(mesh):
    placed = (P(), P("seq", "kv", None), P("seq", "kv", None))
    return jax.shard_map(on_device, mesh=mesh, in_specs=placed, out_specs=P("seq"), check_vma=False)
```

profile of v0, /device:TPU:1, one launch (start us, length us, event | category | flops | bytes accessed | tf_op | source)
XLA Modules:
  0.0 263.4 jit_solution(13679895400350161696)
XLA Ops:
  6.5 0.0 all-gather.2.cloned.1.call-start
  6.5 1.6 copy.10
  8.1 0.0 all-gather.2.cloned.1.call-update
  8.2 1.1 copy.11
  9.3 1.5 fusion.11
  10.7 86.6 %all-gather.2.cloned.1.call-done = bf16[16384,2,128]{2,0,1:T(8,128)(2,1)} async-done(((bf16[256,2,128]{2,0,1:T(8,128)(2,1)}), bf16[16384,2,128]{2,0,1:T(8,128)(2,1)}) %all-gather.2.cloned.1.call-update) | async-done | bytes 8388624 | tf_op jit(solution)/shard_map/all_gather | solution.py:70
  97.4 22.9 %while.22 = (s32[]{:T(128)}, f32[96,2,8]{0,2,1:T(8,128)S(1)}, f32[96,2,8]{0,2,1:T(8,128)S(1)}, s32[8]{0:T(128)S(1)}, s32[]{:T(128)}, /*index=5*/s32[96]{0:T(128)...) while((s32[]{:T(128)}, f32[96,2,8]{0,2,1:T(8,128)S(1)}, ...), condition=%wide.region_6.7_spmd, body=%wide.region_1.6_spmd.sunk | while | flops 830673920 | bytes 27294348 | solution.py:87
  97.4 0.6 dynamic_slice.30
  99.3 7.4 %conditional.4 = ((f32[96,2,8]{0,2,1:T(8,128)S(1)}, f32[96,2,8]{0,2,1:T(8,128)S(1)})) conditional(s32[]{:T(128)} %convert_element_type.8, (f32[96,2,8]{0,2,1:T(8,128)S(1)}, f32[96,2,8]{0,2,1:T(8,128)S(1)}) %tuple.51, (s32[]{:T(128)}, s32[96]{0:T(128)S(1)}, bf16[16384,2,128]{2,0,1:T(8,128)(2,1)}, bf16[96,2,8,128]{3,0,2,1:T(8,128)(2,1)S(1)}, ...), branch_computations={%region_2.2_spmd, %region_3.5_spmd} | conditional | flops 830673920 | bytes 27294146 | solution.py:81
  99.3 0.2 broadcast_compare_fusion
  99.5 3.7 %fusion = (f32[96,2,8]{0,2,1:T(8,128)S(1)}, f32[2,2048,96,8]{1,2,3,0:T(8,128)S(1)}) fusion(pred[96,2048]{1,0:T(8,128)(4,1)S(1)} %broadcast_compare_fusion, bf16[96,2,8,128]{3,0,2,1:T(8,128)(2,1)S(1)} %get-tuple-element.103, bf16[16384,2,128]{2,0,1:T(8,128)(2,1)} %get-tuple-element.102, s32[]{:T(128)S(6)} %select_n.13), kind=kOutput, calls=%fused_computation.2 | convolution fusion | flops 814742016 | bytes 14227460 | tf_op jit(solution)/shard_map/while/body/eval_jaxpr/cond/branch_1_fun/rgid,kgd->rgik/dot_general | solution.py:33
  103.1 3.5 %select_reduce_fusion = f32[96,2,8]{0,2,1:T(8,128)S(1)} fusion(f32[2,2048,96,8]{1,2,3,0:T(8,128)S(1)} %get-tuple-element.171, f32[96,2,8]{0,2,1:T(8,128)S(1)} %max.2, pred[96,2048]{1,0:T(8,128)(4,1)S(1)} %broadcast_compare_fusion), kind=kLoop, calls=%fused_computation.1 | loop fusion | flops 15727104 | bytes 12791808 | tf_op jit(solution)/shard_map/while/body/eval_jaxpr/cond/branch_1_fun/reduce_sum | solution.py:50
  106.7 0.6 dynamic_slice.30
  108.7 0.6 dynamic_slice.30
  110.6 0.6 dynamic_slice.30
  112.5 0.6 dynamic_slice.30
  114.5 0.6 dynamic_slice.30
  116.4 0.6 dynamic_slice.30
  118.4 0.6 dynamic_slice.30
  120.3 22.7 %while.23 = (s32[]{:T(128)}, f32[8,2048]{1,0:T(8,128)S(1)}, s32[8]{0:T(128)S(1)}, s32[]{:T(128)}, s32[96]{0:T(128)S(1)}, /*index=5*/bf16[16384,2,128]{2,0,1:T(8,...) while((s32[]{:T(128)}, f32[8,2048]{1,0:T(8,128)S(1)}, ...), condition=%wide.region_11.12_spmd, body=%wide.region_7.11_spmd.sunk | while | flops 818085888 | bytes 1882737 | solution.py:106
  120.3 0.6 dynamic_slice.31
  122.2 5.4 %conditional.5 = (f32[1,2048]{1,0:T(1,128)S(1)}) conditional(s32[]{:T(128)} %convert_element_type.9, () %tuple.54, (s32[]{:T(128)}, s32[96]{0:T(128)S(1)}, bf16[16384,2,128]{2,0,1:T(8,128)(2,1)}, bf16[96,2,8,128]{3,0,2,1:T(8,128)(2,1)S(1)}, f32[96,2,8]{0,2,1:T(8,128)S(1)}) %tuple.55), branch_computations={%region_8.8_spmd, %region_9.10_spmd} | conditional | flops 818085888 | bytes 1866162 | solution.py:102
  122.3 0.2 broadcast_compare_fusion.1
  122.5 5.1 %fusion.7 = f32[2048]{0:T(1024)S(1)} fusion(f32[96,2,8]{0,2,1:T(8,128)S(1)} %get-tuple-element.120, pred[96,2048]{1,0:T(8,128)(4,1)S(1)} %broadcast_compare_fusion.1, bf16[96,2,8,128]{3,0,2,1:T(8,128)(2,1)S(1)} %get-tuple-element.119, bf16[16384,2,128]{2,0,1:T(8,128)(2,1)} %get-tuple-element.118, s32[]{:T(128)S(6)} %select_n.16), kind=kOutput, calls=%fused_computation.13 | convolution fusion | flops 817887232 | bytes 1652740 | tf_op jit(solution)/shard_map/while/body/eval_jaxpr/cond/branch_1_fun/rgid,kgd->rgik/dot_general | solution.py:33
  127.6 0.2 dynamic_update_slice.5
  127.8 0.6 dynamic_slice.31
  129.8 0.2 dynamic_update_slice.5
  130.0 0.6 dynamic_slice.31
  131.9 0.2 dynamic_update_slice.5
  132.2 0.6 dynamic_slice.31
  134.1 0.2 dynamic_update_slice.5
  134.3 0.6 dynamic_slice.31
  136.3 0.2 dynamic_update_slice.5
  136.5 0.6 dynamic_slice.31
  138.4 0.2 dynamic_update_slice.5
  138.7 0.6 dynamic_slice.31
  140.6 0.2 dynamic_update_slice.5
  140.8 0.6 dynamic_slice.31
  142.8 0.2 dynamic_update_slice.5
  143.0 0.1 all_to_all.10
  143.1 104.8 %all_to_all.15 = f32[64,1,256]{2,1,0:T(1,128)S(1)} all-to-all(f32[64,1,256]{2,1,0:T(1,128)S(1)} %all_to_all.10), channel_id=1, replica_groups=mesh['kv'=4,'seq'=64] {'seq'}, dimensions={0} | all-to-all | bytes 131072 | tf_op jit(solution)/shard_map/all_to_all | solution.py:18
  247.9 0.1 reduce_sum.36
  248.0 8.0 %all_to_all.16 = f32[4,1,256]{2,1,0:T(1,128)S(1)} all-to-all(f32[4,1,256]{2,1,0:T(1,128)S(1)} %broadcast_in_dim.55), channel_id=1, replica_groups=mesh['kv'=4,'seq'=64] {'kv'}, dimensions={0} | all-to-all | bytes 8192 | tf_op jit(solution)/shard_map/all_to_all | solution.py:24
  256.0 0.6 broadcast_multiply_fusion
  (34 shorter events, 0.4 us)
Async XLA Ops:
  6.5 90.8 %all-gather.2.cloned.1.call-start = ((), (), s32[]{:S(2)}) async-start(), calls=%async_computation.2 | async-start | bytes 8519680 | tf_op jit(solution)/shard_map/all_gather | solution.py:70
Sparse Core Ops, SparseCore 0:
  10.2 87.1 all-gather.1
where the time goes:
time: 265 us; the launch traced here: 263 us
  blocking collectives  113 us (43%)
  waiting for transfers between devices  86.6 us (33%)
  loops' own time  21.6 us (8%)
  local copies, waits for them, and re-layouts  14 us (5%)
  between operations  13.5 us (5%)
  matrix products  8.79 us (3%)
  other arithmetic  6.1 us (2%)
    all_to_all x1, blocking collectives, sum_at_owner(): lax.all_to_all(split_up(array, dim, devices), axis, 0, 0, tiled=True)  105 us
    all_gather x1, waiting for transfers between devices, on_device(): gathered = lax.all_gather(key_vectors, 'seq', axis=0, tiled=True)  86.6 us
    another operation x1, loops' own time, terms(): lax.map(portion, jnp.arange(amount // stride, dtype=jnp.int32))  10.7 us
    another operation x1, loops' own time, on_device(): lax.scan(sweep, initial, jnp.arange(total_keys // key_stride, dtype=jnp.i...  10.6 us
    dynamic_slice x16, local copies, waits for them, and re-layouts, on_device(): lax.scan(sweep, initial, jnp.arange(total_keys // key_stride, dtype=jnp.i...  9.59 us
    dot_general x2, matrix products, block_scores(): jnp.einsum('rgid,kgd->rgik', query_block, key_block, preferred_element_ty...  8.79 us
    all_to_all x1, blocking collectives, copy_for_each(): return lax.all_to_all(copies, axis, split_axis=0, concat_axis=0, tiled=True)  7.96 us
  transfers between devices with their start and end apart: 1, of which 1 were waited for; matrix products, arithmetic and copies ran while one was open for 1% of the time, Pallas kernels for 0%

commit v1 on v0

--- a/solution.py
+++ b/solution.py
@@ -67,7 +67,9 @@
     grouped = query_vectors.reshape(local_rows, local_groups, group_size, HD)
     own_rows = lax.dynamic_slice_in_dim(sampled_rows, seq_index * local_rows, local_rows, 0)
     highest = jnp.max(own_rows)
-    gathered = lax.all_gather(key_vectors, "seq", axis=0, tiled=True)
+    gathered = jnp.concatenate(
+        lax.all_to_all(jnp.stack([key_vectors] * lax.axis_size("seq")), "seq", 0, 0), axis=0
+    )
     total_keys = gathered.shape[0]
     key_stride = math.gcd(total_keys, 2048)
 

time: 265 us -> 372 us (1.40)
  waiting for transfers between devices: 86.6 us -> 181 us
  between operations: 13.5 us -> 0.1 us
  starting transfers between devices: 0.01 us -> 13.2 us
  local copies, waits for them, and re-layouts: 14 us -> 25.4 us
    all_to_all x0 -> x1, waiting for transfers between devices: none -> 181 us  [on_device(): lax.all_to_all(jnp.stack([key_vectors] * lax.axis_size('seq')), 'seq', 0, 0)]
    all_gather x1 -> x0, waiting for transfers between devices: 86.6 us -> none  [on_device(): gathered = lax.all_gather(key_vectors, 'seq', axis=0, tiled=True)]
    all_to_all x0 -> x1, starting transfers between devices: none -> 13.2 us  [on_device(): lax.all_to_all(jnp.stack([key_vectors] * lax.axis_size('seq')), 'seq', 0, 0)]
    all_to_all x0 -> x1, local copies, waits for them, and re-layouts: none -> 7.71 us  [on_device(): lax.all_to_all(jnp.stack([key_vectors] * lax.axis_size('seq')), 'seq', 0, 0)]
    another operation x0 -> x1, local copies, waits for them, and re-layouts: none -> 5.31 us  [on_device(): jnp.stack([key_vectors] * lax.axis_size('seq'))]
  transfers between devices with their start and end apart: 1 -> 1, of which waited for: 1 -> 1; matrix products, arithmetic and copies ran while one was open for 1% -> 0% of each run, Pallas kernels for 0% -> 0%
where the time goes in v1:
time: 372 us; the launch traced here: 370 us
  waiting for transfers between devices  181 us (49%)
  blocking collectives  116 us (31%)
  local copies, waits for them, and re-layouts  25.4 us (7%)
  loops' own time  19.8 us (5%)
  starting transfers between devices  13.2 us (4%)
  matrix products  8.79 us (2%)
  other arithmetic  6.03 us (2%)
    all_to_all x1, waiting for transfers between devices, on_device(): lax.all_to_all(jnp.stack([key_vectors] * lax.axis_size('seq')), 'seq', 0, 0)  181 us
    all_to_all x1, blocking collectives, sum_at_owner(): lax.all_to_all(split_up(array, dim, devices), axis, 0, 0, tiled=True)  108 us
    all_to_all x1, starting transfers between devices, on_device(): lax.all_to_all(jnp.stack([key_vectors] * lax.axis_size('seq')), 'seq', 0, 0)  13.2 us
    another operation x1, loops' own time, terms(): lax.map(portion, jnp.arange(amount // stride, dtype=jnp.int32))  9.8 us
    another operation x1, loops' own time, on_device(): lax.scan(sweep, initial, jnp.arange(total_keys // key_stride, dtype=jnp.i...  9.73 us
    dynamic_slice x16, local copies, waits for them, and re-layouts, on_device(): lax.scan(sweep, initial, jnp.arange(total_keys // key_stride, dtype=jnp.i...  9.59 us
    dot_general x2, matrix products, block_scores(): jnp.einsum('rgid,kgd->rgik', query_block, key_block, preferred_element_ty...  8.79 us
    all_to_all x1, blocking collectives, copy_for_each(): return lax.all_to_all(copies, axis, split_axis=0, concat_axis=0, tiled=True)  8.12 us
  transfers between devices with their start and end apart: 1, of which 1 were waited for; matrix products, arithmetic and copies ran while one was open for 0% of the time, Pallas kernels for 0%

profile of v1, /device:TPU:1, one launch (start us, length us, event | category | flops | bytes accessed | tf_op | source)
XLA Modules:
  0.0 370.5 jit_solution(15703312049944045497)
XLA Ops:
  0.0 0.9 copy.14
  0.9 0.0 copy-start
  0.9 5.3 %stack.2 = bf16[64,256,2,128]{3,1,2,0:T(8,128)(2,1)} broadcast(bf16[256,2,128]{2,0,1:T(8,128)(2,1)S(1)} %copy.14), dimensions={1,2,3} | broadcast | bytes 8519680 | tf_op jit(solution)/shard_map/stack | solution.py:71
  6.3 13.2 %all-to-all-start = ((bf16[64,256,2,128]{3,1,2,0:T(8,128)(2,1)}), bf16[64,256,2,128]{3,1,2,0:T(8,128)(2,1)}, u32[]{:S(2)}, u32[]{:S(2)}) async-start(bf16[64,256,2,128]{3,1,2,0:T(8,128)(2,1)} %stack.2), calls=%async_computation | async-start | bytes 16777216 | tf_op jit(solution)/shard_map/all_to_all | solution.py:71
  19.5 0.0 copy-done
  19.5 0.1 copy.16
  19.6 1.4 fusion.11
  21.0 180.8 %all-to-all-done = bf16[64,256,2,128]{3,1,2,0:T(8,128)(2,1)} async-done(((bf16[64,256,2,128]{3,1,2,0:T(8,128)(2,1)}), bf16[64,256,2,128]{3,1,2,0:T(8,128)(2,1)}, u32[]{:S(2)}, u32[]{:S(2)}) %all-to-all-start) | async-done | bytes 8388640 | tf_op jit(solution)/shard_map/all_to_all | solution.py:71
  201.8 7.7 %copy.15 = bf16[64,256,2,128]{3,1,0,2:T(8,128)(2,1)} copy(bf16[64,256,2,128]{3,1,2,0:T(8,128)(2,1)} %all-to-all-done) | data formatting | bytes 16777216 | tf_op jit(solution)/shard_map/all_to_all | solution.py:71
  209.5 22.0 %while.22 = (s32[]{:T(128)}, f32[96,2,8]{0,2,1:T(8,128)S(1)}, f32[96,2,8]{0,2,1:T(8,128)S(1)}, s32[8]{0:T(128)S(1)}, s32[]{:T(128)}, /*index=5*/s32[96]{0:T(128)...) while((s32[]{:T(128)}, f32[96,2,8]{0,2,1:T(8,128)S(1)}, ...), condition=%wide.region_6.7_spmd, body=%wide.region_1.6_spmd.sunk | while | flops 830673920 | bytes 27294348 | solution.py:89
  209.5 0.6 dynamic_slice.30
  211.3 7.5 %conditional.4 = ((f32[96,2,8]{0,2,1:T(8,128)S(1)}, f32[96,2,8]{0,2,1:T(8,128)S(1)})) conditional(s32[]{:T(128)} %convert_element_type.8, (f32[96,2,8]{0,2,1:T(8,128)S(1)}, f32[96,2,8]{0,2,1:T(8,128)S(1)}) %tuple.51, (s32[]{:T(128)}, s32[96]{0:T(128)S(1)}, bf16[16384,2,128]{2,0,1:T(8,128)(2,1)}, bf16[96,2,8,128]{3,0,2,1:T(8,128)(2,1)S(1)}, ...), branch_computations={%region_2.2_spmd, %region_3.5_spmd} | conditional | flops 830673920 | bytes 27294146 | solution.py:83
  211.4 0.2 broadcast_compare_fusion
  211.5 3.7 fusion
  215.2 3.5 select_reduce_fusion
  218.8 0.6 dynamic_slice.30
  220.6 0.6 dynamic_slice.30
  222.5 0.6 dynamic_slice.30
  224.3 0.6 dynamic_slice.30
  226.1 0.6 dynamic_slice.30
  227.9 0.6 dynamic_slice.30
  229.8 0.6 dynamic_slice.30
  231.6 21.8 %while.23 = (s32[]{:T(128)}, f32[8,2048]{1,0:T(8,128)S(1)}, s32[8]{0:T(128)S(1)}, s32[]{:T(128)}, s32[96]{0:T(128)S(1)}, /*index=5*/bf16[16384,2,128]{2,0,1:T(8,...) while((s32[]{:T(128)}, f32[8,2048]{1,0:T(8,128)S(1)}, ...), condition=%wide.region_11.12_spmd, body=%wide.region_7.11_spmd.sunk | while | flops 818085888 | bytes 1882737 | solution.py:108
  231.6 0.6 dynamic_slice.31
  233.4 5.4 %conditional.5 = (f32[1,2048]{1,0:T(1,128)S(1)}) conditional(s32[]{:T(128)} %convert_element_type.9, () %tuple.54, (s32[]{:T(128)}, s32[96]{0:T(128)S(1)}, bf16[16384,2,128]{2,0,1:T(8,128)(2,1)}, bf16[96,2,8,128]{3,0,2,1:T(8,128)(2,1)S(1)}, f32[96,2,8]{0,2,1:T(8,128)S(1)}) %tuple.55), branch_computations={%region_8.8_spmd, %region_9.10_spmd} | conditional | flops 818085888 | bytes 1866162 | solution.py:104
  233.5 0.2 broadcast_compare_fusion.1
  233.6 5.1 %fusion.7 = f32[2048]{0:T(1024)S(1)} fusion(f32[96,2,8]{0,2,1:T(8,128)S(1)} %get-tuple-element.120, pred[96,2048]{1,0:T(8,128)(4,1)S(1)} %broadcast_compare_fusion.1, bf16[96,2,8,128]{3,0,2,1:T(8,128)(2,1)S(1)} %get-tuple-element.119, bf16[16384,2,128]{2,0,1:T(8,128)(2,1)} %get-tuple-element.118, s32[]{:T(128)S(6)} %select_n.16), kind=kOutput, calls=%fused_computation.13 | convolution fusion | flops 817887232 | bytes 1652740 | tf_op jit(solution)/shard_map/while/body/eval_jaxpr/cond/branch_1_fun/rgid,kgd->rgik/dot_general | solution.py:33
  238.8 0.2 dynamic_update_slice.5
  239.0 0.6 dynamic_slice.31
  240.8 0.2 dynamic_update_slice.5
  241.1 0.6 dynamic_slice.31
  242.9 0.2 dynamic_update_slice.5
  243.1 0.6 dynamic_slice.31
  244.9 0.2 dynamic_update_slice.5
  245.2 0.6 dynamic_slice.31
  247.0 0.2 dynamic_update_slice.5
  247.2 0.6 dynamic_slice.31
  249.1 0.2 dynamic_update_slice.5
  249.3 0.6 dynamic_slice.31
  251.1 0.2 dynamic_update_slice.5
  251.3 0.6 dynamic_slice.31
  253.2 0.2 dynamic_update_slice.5
  253.4 0.1 all_to_all.14
  253.5 108.2 %all_to_all.20 = f32[64,1,256]{2,1,0:T(1,128)S(1)} all-to-all(f32[64,1,256]{2,1,0:T(1,128)S(1)} %all_to_all.14), channel_id=1, replica_groups=mesh['kv'=4,'seq'=64] {'seq'}, dimensions={0} | all-to-all | bytes 131072 | tf_op jit(solution)/shard_map/all_to_all | solution.py:18
  361.7 0.1 reduce_sum.36
  361.8 8.1 %all_to_all.21 = f32[4,1,256]{2,1,0:T(1,128)S(1)} all-to-all(f32[4,1,256]{2,1,0:T(1,128)S(1)} %broadcast_in_dim.55), channel_id=1, replica_groups=mesh['kv'=4,'seq'=64] {'kv'}, dimensions={0} | all-to-all | bytes 8192 | tf_op jit(solution)/shard_map/all_to_all | solution.py:24
  369.9 0.6 broadcast_multiply_fusion
  (34 shorter events, 0.4 us)
Async XLA Ops:
  0.9 18.5 %copy-start = (bf16[96,16,128]{2,1,0:T(8,128)(2,1)S(1)}, bf16[96,16,128]{2,1,0:T(8,128)(2,1)}, u32[]{:S(2)}) copy-start(bf16[96,16,128]{2,1,0:T(8,128)(2,1)} %param.12) | copy-start | bytes 1179652
  6.3 195.6 %all-to-all-start = ((bf16[64,256,2,128]{3,1,2,0:T(8,128)(2,1)}), bf16[64,256,2,128]{3,1,2,0:T(8,128)(2,1)}, u32[]{:S(2)}, u32[]{:S(2)}) async-start(bf16[64,256,2,128]{3,1,2,0:T(8,128)(2,1)} %stack.2), calls=%async_computation | async-start | bytes 16777216 | tf_op jit(solution)/shard_map/all_to_all | solution.py:71
